TPU v7x, 256 devices: a whole 4x4x8 slice. The times are simulated.
256 devices in a mesh: freq: 16 (over x, z_hi), tile: 16 (over z_lo, y, core).
Axes of the slice: x: 4, y: 4, z: 8 (z_hi: 4, z_lo: 2; z = z_hi * 2 + z_lo), core: 2. Of those that a mesh axis runs over, the one named last changes fastest.
Arguments:
- sky_cube: float32 [256, 256, 128], P(('freq', 'tile')), may hold values from -6 to 6
- kernel_one: bfloat16 [8, 1, 3, 3, 3], replicated, may hold values from -1.25 to 1.25
- bias_one: float32 [8], replicated, may hold values from -2 to 2
- kernel_two: bfloat16 [8, 8, 3, 3, 3], replicated, may hold values from -0.4375 to 0.4375
- bias_two: float32 [8], replicated, may hold values from -2 to 2
- kernel_three: bfloat16 [16, 8, 3, 3, 3], replicated, may hold values from -0.4375 to 0.4375
- bias_three: float32 [16], replicated, may hold values from -2 to 2
Outputs:
- features: bfloat16 [16, 128, 128, 64], P(None, 'freq', 'tile')
All inputs are finite; a program needn't handle non-finite values.
Results may differ from a plain program's by a relative error of at most 0.0066.
Values may be sent and summed in bfloat16 or wider, within the bound.
A program may use at most 64 MiB of HBM per device.

v0:
```python
import jax
import jax.numpy as jnp
from jax import lax
from jax.sharding import PartitionSpec as P


def extended_2(cells, sides, width):
    for axis, dim in sides:
        count = lax.axis_size(axis)
        ends = count - 1
        head = lax.slice_in_dim(cells, 0, width, axis=dim)
        tail = lax.slice_in_dim(cells, cells.shape[dim] - width, cells.shape[dim], axis=dim)
        cells = jnp.concatenate(
            [
                lax.ppermute(tail, axis, [(i, (i + 1) % count) for i in range(ends)]),
                cells,
                lax.ppermute(head, axis, [((i + 1) % count, i) for i in range(ends)]),
            ],
            axis=dim,
        )
    return cells


def shortened(shard):

    def short(part):
        return part.astype(jnp.bfloat16) if part.dtype == jnp.float32 else part

    return jax.tree.map(short, shard)


def from_behind(shard, axis, by):
    devices = lax.axis_size(axis)
    pairs = [(i, i + by) for i in range(devices) if 0 <= i + by < devices]
    return lax.ppermute(shard, axis, pairs)


def leaky_relu(values):
    return jnp.maximum(values, 0.1 * values)


def conv_layer(volume, kernel, bias_term):
    depth = volume.shape[1] - 2
    blocks = []
    for begin_at in range(0, depth, 4):
        count = min(4, depth - begin_at)
        section = volume[:, begin_at : begin_at + count + 2]
        values = lax.conv_general_dilated(
            section[None],
            kernel,
            (1, 1, 1),
            ((0, 0), (0, 0), (1, 1)),
            dimension_numbers=("NCDHW", "OIDHW", "NCDHW"),
            preferred_element_type=jnp.float32,
        )[0]
        values = leaky_relu(values + bias_term[:, None, None, None])
        blocks.append(values.astype(jnp.bfloat16))
    return jnp.concatenate(blocks, axis=1)


def body(sky_cube, kernel_one, bias_one, kernel_two, bias_two, kernel_three, bias_three):
    slab = lax.all_to_all(
        sky_cube.astype(jnp.bfloat16), "tile", split_axis=1, concat_axis=0, tiled=True
    )
    widened = extended_2(slab, (("freq", 0), ("tile", 1)), 1)
    layer_one = conv_layer(widened[None], kernel_one, bias_one)
    widened = extended_2(layer_one, (("freq", 1), ("tile", 2)), 1)
    layer_two = conv_layer(widened, kernel_two, bias_two)
    lower_rows = from_behind(shortened(layer_two[:, :, -1:, :]), "tile", 1)
    extended = jnp.concatenate([lower_rows, layer_two], axis=2)
    lower_planes = from_behind(shortened(extended[:, -1:]), "freq", 1)
    extended = jnp.concatenate([lower_planes, extended], axis=1)
    values = lax.conv_general_dilated(
        extended[None],
        kernel_three,
        (2, 2, 2),
        ((0, 0), (0, 0), (1, 1)),
        dimension_numbers=("NCDHW", "OIDHW", "NCDHW"),
        preferred_element_type=jnp.float32,
    )[0]
    return leaky_relu(values + bias_three[:, None, None, None]).astype(jnp.bfloat16)


def solution(mesh):
    return jax.shard_map(
        body,
        mesh=mesh,
        in_specs=(P(("freq", "tile"), None, None), P(), P(), P(), P(), P(), P()),
        out_specs=P(None, "freq", "tile", None),
        check_vma=False,
    )
```

profile of v0, /device:TPU:34, one launch (start us, length us, event | category | flops | bytes accessed | tf_op | source)
XLA Modules:
  0.0 293.2 jit_solution(5028507617221354503)
XLA Ops:
  0.0 0.9 convert_element_type.30
  1.5 1.0 reduce
  2.6 10.6 %all_to_all.15 = bf16[16,2,1024]{2,1,0:T(2,128)(2,1)S(1)} all-to-all(bf16[16,2,1024]{2,1,0:T(2,128)(2,1)S(1)} %reshape.116), channel_id=1, replica_groups=mesh['freq'=16,'tile'=16] {'tile'}, dimensions={0} | all-to-all | bytes 131072 | tf_op jit(solution)/shard_map/all_to_all | solution.py:62
  13.3 5.2 %collective-permute-start = (bf16[1,16,128]{2,1,0:T(8,128)(2,1)S(1)}, bf16[1,16,128]{2,1,0:T(8,128)(2,1)S(1)}, u32[]{:S(2)}, u32[]{:S(2)}) collective-permute-start(bf16[1,16,128]{2,1,0:T(8,128)(2,1)S(1)} %slice_bitcast_fusion.16), channel_id=1, source_target_pairs={{0,16},{16,32},{32,48},{48,64},{64,80},{80,96},{96,112},{112,128},... | collective-permute-start | bytes 12296 | tf_op jit(solution)/shard_map/ppermute | solution.py:15
  18.5 4.0 %collective-permute-start.1 = (bf16[1,16,128]{2,1,0:T(8,128)(2,1)S(1)}, bf16[1,16,128]{2,1,0:T(8,128)(2,1)S(1)}, u32[]{:S(2)}, u32[]{:S(2)}) collective-permute-start(bf16[1,16,128]{2,1,0:T(8,128)(2,1)S(1)} %copy.172), channel_id=1, source_target_pairs={{16,0},{32,16},{48,32},{64,48},{80,64},{96,80},{112,96},{128,112},... | collective-permute-start | bytes 12296 | tf_op jit(solution)/shard_map/ppermute | solution.py:17
  22.5 3.0 %collective-permute-done.1 = bf16[1,16,128]{2,1,0:T(8,128)(2,1)S(1)} collective-permute-done((bf16[1,16,128]{2,1,0:T(8,128)(2,1)S(1)}, bf16[1,16,128]{2,1,0:T(8,128)(2,1)S(1)}, u32[]{:S(2)}, u32[]{:S(2)}) %collective-permute-start.1) | collective-permute-done | bytes 4128 | tf_op jit(solution)/shard_map/ppermute | solution.py:17
  25.6 1.9 collective-permute-start.2
  27.5 5.8 %collective-permute-start.3 = (bf16[18,1,128]{2,1,0:T(2,128)(2,1)S(1)}, bf16[18,1,128]{2,1,0:T(2,128)(2,1)S(1)}, u32[]{:S(2)}, u32[]{:S(2)}) collective-permute-start(bf16[18,1,128]{2,1,0:T(2,128)(2,1)S(1)} %get-tuple-element.18), channel_id=1, source_target_pairs={{1,0},{2,1},{3,2},{4,3},{5,4},{6,5},{7,6},{8,7},{9,8},{10,9},{11,1... | collective-permute-start | bytes 13832 | tf_op jit(solution)/shard_map/ppermute | solution.py:17
  33.3 1.3 collective-permute-done.3
  36.9 2.2 copy.142
  39.0 2.6 copy.145
  41.6 1.6 copy.148
  43.2 1.7 copy.151
  44.9 8.6 %broadcast_select_fusion.4 = f32[4,16,8,17,8]{4,2,3,1,0:T(8,128)} fusion(pred[8,17]{0,1:T(8,128)(4,1)S(1)} %copy-done.6, bf16[1,6,18,8,19]{3,0,4,2,1:T(2,128)(2,1)S(1)} %copy.151, bf16[8,1,3,3,3]{0,4,3,2,1:T(4,128)(2,1)S(1)} %copy-done.5), kind=kOutput, calls=%fused_computation.39 | convolution fusion | flops 3829760 | bytes 311928 | tf_op jit(solution)/shard_map/conv_general_dilated | solution.py:48
  53.6 8.7 %broadcast_select_fusion.5 = f32[4,16,8,17,8]{4,2,3,1,0:T(8,128)} fusion(pred[8,17]{0,1:T(8,128)(4,1)S(1)} %copy-done.6, bf16[1,6,18,8,19]{3,0,4,2,1:T(2,128)(2,1)S(1)} %copy.148, bf16[8,1,3,3,3]{0,4,3,2,1:T(4,128)(2,1)S(1)} %copy-done.5), kind=kOutput, calls=%fused_computation.40 | convolution fusion | flops 3829760 | bytes 311928 | tf_op jit(solution)/shard_map/conv_general_dilated | solution.py:48
  62.3 8.8 %broadcast_select_fusion.7 = f32[4,16,8,17,8]{4,2,3,1,0:T(8,128)} fusion(pred[8,17]{0,1:T(8,128)(4,1)S(1)} %copy-done.6, bf16[1,6,18,8,19]{3,0,4,2,1:T(2,128)(2,1)S(1)} %copy.142, bf16[8,1,3,3,3]{0,4,3,2,1:T(4,128)(2,1)S(1)} %copy-done.5), kind=kOutput, calls=%fused_computation.42 | convolution fusion | flops 3829760 | bytes 311928 | tf_op jit(solution)/shard_map/conv_general_dilated | solution.py:48
  71.0 5.4 %copy.144 = f32[4,16,8,17,8]{3,2,4,1,0:T(8,128)S(1)} copy(f32[4,16,8,17,8]{4,2,3,1,0:T(8,128)} %broadcast_select_fusion.7) | data formatting | bytes 557056 | tf_op jit(solution)/shard_map/conv_general_dilated | solution.py:48
  77.1 6.0 %collective-permute-start.4 = (bf16[8,1,16,128]{3,0,2,1:T(8,128)(2,1)S(1)}, bf16[8,1,16,128]{3,0,2,1:T(8,128)(2,1)S(1)}, u32[]{:S(2)}, u32[]{:S(2)}) collective-permute-start(bf16[8,1,16,128]{3,0,2,1:T(8,128)(2,1)S(1)} %slice.100), channel_id=1, source_target_pairs={{0,16},{16,32},{32,48},{48,64},{64,80},{80,96},{96,112},{112,128},... | collective-permute-start | bytes 98312 | tf_op jit(solution)/shard_map/ppermute | solution.py:15
  83.2 9.6 %broadcast_select_fusion.6 = f32[4,16,8,17,8]{4,2,3,1,0:T(8,128)} fusion(pred[8,17]{0,1:T(8,128)(4,1)S(1)} %copy-done.6, bf16[1,6,18,8,19]{3,0,4,2,1:T(2,128)(2,1)} %copy.145, bf16[8,1,3,3,3]{0,4,3,2,1:T(4,128)(2,1)S(1)} %copy-done.5), kind=kOutput, calls=%fused_computation.41 | convolution fusion | flops 3829760 | bytes 311928 | tf_op jit(solution)/shard_map/conv_general_dilated | solution.py:48
  92.7 5.2 %copy.153 = f32[4,16,8,17,8]{3,2,4,1,0:T(8,128)S(1)} copy(f32[4,16,8,17,8]{4,2,3,1,0:T(8,128)} %broadcast_select_fusion.4) | data formatting | bytes 557056 | tf_op jit(solution)/shard_map/conv_general_dilated | solution.py:48
  97.9 1.4 reshape.35
  99.3 5.2 %copy.150 = f32[4,16,8,17,8]{3,2,4,1,0:T(8,128)S(1)} copy(f32[4,16,8,17,8]{4,2,3,1,0:T(8,128)} %broadcast_select_fusion.5) | data formatting | bytes 557056 | tf_op jit(solution)/shard_map/conv_general_dilated | solution.py:48
  104.5 1.4 reshape.28
  105.9 5.2 %copy.147 = f32[4,16,8,17,8]{3,2,4,1,0:T(8,128)S(1)} copy(f32[4,16,8,17,8]{4,2,3,1,0:T(8,128)} %broadcast_select_fusion.6) | data formatting | bytes 557056 | tf_op jit(solution)/shard_map/conv_general_dilated | solution.py:48
  111.8 2.8 collective-permute-start.5
  114.7 1.1 fusion.83
  115.7 1.1 fusion.82
  117.0 1.6 collective-permute-done.5
  118.6 1.9 collective-permute-start.6
  120.5 5.8 %collective-permute-start.7 = (bf16[8,18,1,128]{3,0,2,1:T(8,128)(2,1)S(1)}, bf16[8,18,1,128]{3,0,2,1:T(8,128)(2,1)S(1)}, u32[]{:S(2)}, u32[]{:S(2)}) collective-permute-start(bf16[8,18,1,128]{3,0,2,1:T(8,128)(2,1)S(1)} %get-tuple-element.12), channel_id=1, source_target_pairs={{1,0},{2,1},{3,2},{4,3},{5,4},{6,5},{7,6},{8,7},{9,8},{10,9},{11,1... | collective-permute-start | bytes 110600 | tf_op jit(solution)/shard_map/ppermute | solution.py:17
  126.3 1.6 collective-permute-done.7
  128.9 2.4 reshape.45
  131.3 2.2 reshape.52
  133.5 2.3 reshape.59
  135.8 1.3 reshape.38
  137.1 6.7 %copy.155 = bf16[8,6,18,1,8,17]{0,4,5,2,1,3:T(8,128)(2,1)} copy(bf16[8,6,18,1,8,17]{5,4,0,2,1,3:T(8,128)(2,1)S(1)} %reshape.38) | data formatting | bytes 470016 | tf_op jit(solution)/shard_map/conv_general_dilated | solution.py:48
  143.8 1.1 slice.114
  144.9 9.7 %broadcast_select_fusion.3 = f32[4,16,8,17,8]{4,2,3,1,0:T(8,128)} fusion(pred[8,17]{0,1:T(8,128)(4,1)S(1)} %copy-done.6, bf16[8,8,3,3,3]{1,0,4,3,2:T(8,128)(2,1)S(1)} %copy-done, bf16[8,6,18,1,7,2]{0,4,5,2,1,3:T(8,128)(2,1)S(1)} %slice.114, bf16[8,6,18,1,8,17]{0,4,5,2,1,3:T(8,128)(2,1)} %copy.155), kind=kOutput, calls=%fused_computation.38 | convolution fusion | flops 30938624 | bytes 541320 | tf_op jit(solution)/shard_map/conv_general_dilated | solution.py:48
  154.7 5.2 %copy.156 = f32[4,16,8,17,8]{3,2,4,1,0:T(8,128)S(1)} copy(f32[4,16,8,17,8]{4,2,3,1,0:T(8,128)} %broadcast_select_fusion.3) | data formatting | bytes 557056 | tf_op jit(solution)/shard_map/conv_general_dilated | solution.py:48
  160.5 7.5 %copy.164 = bf16[8,6,18,1,8,17]{0,4,5,2,1,3:T(8,128)(2,1)} copy(bf16[8,6,18,1,8,17]{5,4,0,2,1,3:T(8,128)(2,1)} %reshape.59) | data formatting | bytes 470016 | tf_op jit(solution)/shard_map/conv_general_dilated | solution.py:48
  168.0 1.1 slice.123
  169.1 9.7 %broadcast_select_fusion = f32[4,16,8,17,8]{4,2,3,1,0:T(8,128)} fusion(pred[8,17]{0,1:T(8,128)(4,1)S(1)} %copy-done.6, bf16[8,8,3,3,3]{1,0,4,3,2:T(8,128)(2,1)S(1)} %copy-done, bf16[8,6,18,1,7,2]{0,4,5,2,1,3:T(8,128)(2,1)S(1)} %slice.123, bf16[8,6,18,1,8,17]{0,4,5,2,1,3:T(8,128)(2,1)} %copy.164), kind=kOutput, calls=%fused_computation.35 | convolution fusion | flops 30938624 | bytes 541320 | tf_op jit(solution)/shard_map/conv_general_dilated | solution.py:48
  178.9 5.6 %copy.165 = f32[4,16,8,17,8]{3,2,4,1,0:T(8,128)S(1)} copy(f32[4,16,8,17,8]{4,2,3,1,0:T(8,128)} %broadcast_select_fusion) | data formatting | bytes 557056 | tf_op jit(solution)/shard_map/conv_general_dilated | solution.py:48
  185.1 7.5 %copy.161 = bf16[8,6,18,1,8,17]{0,4,5,2,1,3:T(8,128)(2,1)} copy(bf16[8,6,18,1,8,17]{5,4,0,2,1,3:T(8,128)(2,1)} %reshape.52) | data formatting | bytes 470016 | tf_op jit(solution)/shard_map/conv_general_dilated | solution.py:48
  192.6 1.1 slice.120
  193.7 9.7 %broadcast_select_fusion.1 = f32[4,16,8,17,8]{4,2,3,1,0:T(8,128)} fusion(pred[8,17]{0,1:T(8,128)(4,1)S(1)} %copy-done.6, bf16[8,8,3,3,3]{1,0,4,3,2:T(8,128)(2,1)S(1)} %copy-done, bf16[8,6,18,1,7,2]{0,4,5,2,1,3:T(8,128)(2,1)S(1)} %slice.120, bf16[8,6,18,1,8,17]{0,4,5,2,1,3:T(8,128)(2,1)} %copy.161), kind=kOutput, calls=%fused_computation.36 | convolution fusion | flops 30938624 | bytes 541320 | tf_op jit(solution)/shard_map/conv_general_dilated | solution.py:48
  203.5 5.2 %copy.162 = f32[4,16,8,17,8]{3,2,4,1,0:T(8,128)S(1)} copy(f32[4,16,8,17,8]{4,2,3,1,0:T(8,128)} %broadcast_select_fusion.1) | data formatting | bytes 557056 | tf_op jit(solution)/shard_map/conv_general_dilated | solution.py:48
  208.7 1.4 reshape.56
  210.1 7.5 %copy.158 = bf16[8,6,18,1,8,17]{0,4,5,2,1,3:T(8,128)(2,1)} copy(bf16[8,6,18,1,8,17]{5,4,0,2,1,3:T(8,128)(2,1)} %reshape.45) | data formatting | bytes 470016 | tf_op jit(solution)/shard_map/conv_general_dilated | solution.py:48
  217.6 1.1 slice.117
  218.7 9.7 %broadcast_select_fusion.2 = f32[4,16,8,17,8]{4,2,3,1,0:T(8,128)} fusion(pred[8,17]{0,1:T(8,128)(4,1)S(1)} %copy-done.6, bf16[8,8,3,3,3]{1,0,4,3,2:T(8,128)(2,1)S(1)} %copy-done, bf16[8,6,18,1,7,2]{0,4,5,2,1,3:T(8,128)(2,1)S(1)} %slice.117, bf16[8,6,18,1,8,17]{0,4,5,2,1,3:T(8,128)(2,1)} %copy.158), kind=kOutput, calls=%fused_computation.37 | convolution fusion | flops 30938624 | bytes 541320 | tf_op jit(solution)/shard_map/conv_general_dilated | solution.py:48
  228.5 5.2 %copy.159 = f32[4,16,8,17,8]{3,2,4,1,0:T(8,128)S(1)} copy(f32[4,16,8,17,8]{4,2,3,1,0:T(8,128)} %broadcast_select_fusion.2) | data formatting | bytes 557056 | tf_op jit(solution)/shard_map/conv_general_dilated | solution.py:48
  233.7 1.4 reshape.49
  235.1 1.3 fusion.62
  236.3 1.9 collective-permute-start.8
  238.3 5.8 %collective-permute-done.8 = bf16[8,16,1,128]{3,0,2,1:T(8,128)(2,1)S(1)} collective-permute-done((bf16[8,16,1,128]{3,0,2,1:T(8,128)(2,1)S(1)}, bf16[8,16,1,128]{3,0,2,1:T(8,128)(2,1)S(1)}, u32[]{:S(2)}, u32[]{:S(2)}) %collective-permute-start.8) | collective-permute-done | bytes 32800 | tf_op jit(solution)/shard_map/ppermute | solution.py:35
  244.1 3.2 %collective-permute-start.9 = (bf16[8,1,17,128]{3,0,2,1:T(8,128)(2,1)S(1)}, bf16[8,1,17,128]{3,0,2,1:T(8,128)(2,1)S(1)}, u32[]{:S(2)}, u32[]{:S(2)}) collective-permute-start(bf16[8,1,17,128]{3,0,2,1:T(8,128)(2,1)S(1)} %pad_maximum_fusion.1), channel_id=1, source_target_pairs={{0,16},{16,32},{32,48},{48,64},{64,80},{80,96},{96,112},{112,128},... | collective-permute-start | bytes 104456 | tf_op jit(solution)/shard_map/ppermute | solution.py:35
  247.2 5.6 %collective-permute-done.9 = bf16[8,1,17,128]{3,0,2,1:T(8,128)(2,1)S(1)} collective-permute-done((bf16[8,1,17,128]{3,0,2,1:T(8,128)(2,1)S(1)}, bf16[8,1,17,128]{3,0,2,1:T(8,128)(2,1)S(1)}, u32[]{:S(2)}, u32[]{:S(2)}) %collective-permute-start.9) | collective-permute-done | bytes 34848 | tf_op jit(solution)/shard_map/ppermute | solution.py:35
  253.4 5.7 %reshape.66 = bf16[8,17,17,1,8,18]{5,4,0,2,1,3:T(8,128)(2,1)} reshape(bf16[8,17,17,1,144]{4,0,2,1,3:T(8,128)(2,1)S(1)} %pad.16) | data formatting | bytes 1331712 | tf_op jit(solution)/shard_map/conv_general_dilated | solution.py:73
  259.1 18.6 %copy.167 = bf16[8,17,17,1,8,18]{0,4,5,2,1,3:T(8,128)(2,1)} copy(bf16[8,17,17,1,8,18]{5,4,0,2,1,3:T(8,128)(2,1)} %reshape.66) | data formatting | bytes 1331712 | tf_op jit(solution)/shard_map/conv_general_dilated | solution.py:73
  277.7 1.6 slice.125
  279.3 11.3 %fusion.50 = f32[8,8,8,9,16]{4,2,3,1,0:T(8,128)S(1)} fusion(bf16[16,8,3,3,3]{0,1,4,3,2:T(8,128)(2,1)S(1)} %copy-done.4, bf16[8,17,17,1,7,2]{0,4,5,2,1,3:T(8,128)(2,1)S(1)} %slice.125, bf16[8,17,17,1,8,18]{0,4,5,2,1,3:T(8,128)(2,1)} %copy.167, pred[8,9]{0,1:T(8,128)(4,1)S(1)} %copy-done.7), kind=kOutput, calls=%fused_computation.47 | convolution fusion | flops 34143744 | bytes 1032488 | tf_op jit(solution)/shard_map/conv_general_dilated | solution.py:73
  291.3 0.8 copy.173
  292.1 0.8 fusion.53
  (71 shorter events, 7.6 us)
Async XLA Ops:
  0.0 144.9 %copy-start = (bf16[8,8,3,3,3]{1,0,4,3,2:T(8,128)(2,1)S(1)}, bf16[8,8,3,3,3]{1,0,4,3,2:T(8,128)(2,1)}, u32[]{:S(2)}) copy-start(bf16[8,8,3,3,3]{1,0,4,3,2:T(8,128)(2,1)} %param.10) | copy-start | bytes 10372
  13.3 9.2 %collective-permute-start = (bf16[1,16,128]{2,1,0:T(8,128)(2,1)S(1)}, bf16[1,16,128]{2,1,0:T(8,128)(2,1)S(1)}, u32[]{:S(2)}, u32[]{:S(2)}) collective-permute-start(bf16[1,16,128]{2,1,0:T(8,128)(2,1)S(1)} %slice_bitcast_fusion.16), channel_id=1, source_target_pairs={{0,16},{16,32},{32,48},{48,64},{64,80},{80,96},{96,112},{112,128},... | collective-permute-start | bytes 12296 | tf_op jit(solution)/shard_map/ppermute | solution.py:15
  18.5 7.1 %collective-permute-start.1 = (bf16[1,16,128]{2,1,0:T(8,128)(2,1)S(1)}, bf16[1,16,128]{2,1,0:T(8,128)(2,1)S(1)}, u32[]{:S(2)}, u32[]{:S(2)}) collective-permute-start(bf16[1,16,128]{2,1,0:T(8,128)(2,1)S(1)} %copy.172), channel_id=1, source_target_pairs={{16,0},{32,16},{48,32},{64,48},{80,64},{96,80},{112,96},{128,112},... | collective-permute-start | bytes 12296 | tf_op jit(solution)/shard_map/ppermute | solution.py:17
  25.6 7.7 %collective-permute-start.2 = (bf16[18,1,128]{2,1,0:T(2,128)(2,1)S(1)}, bf16[18,1,128]{2,1,0:T(2,128)(2,1)S(1)}, u32[]{:S(2)}, u32[]{:S(2)}) collective-permute-start(bf16[18,1,128]{2,1,0:T(2,128)(2,1)S(1)} %get-tuple-element.17), channel_id=1, source_target_pairs={{0,1},{1,2},{2,3},{3,4},{4,5},{5,6},{6,7},{7,8},{8,9},{9,10},{10,1... | collective-permute-start | bytes 13832 | tf_op jit(solution)/shard_map/ppermute | solution.py:15
  27.5 7.1 %collective-permute-start.3 = (bf16[18,1,128]{2,1,0:T(2,128)(2,1)S(1)}, bf16[18,1,128]{2,1,0:T(2,128)(2,1)S(1)}, u32[]{:S(2)}, u32[]{:S(2)}) collective-permute-start(bf16[18,1,128]{2,1,0:T(2,128)(2,1)S(1)} %get-tuple-element.18), channel_id=1, source_target_pairs={{1,0},{2,1},{3,2},{4,3},{5,4},{6,5},{7,6},{8,7},{9,8},{10,9},{11,1... | collective-permute-start | bytes 13832 | tf_op jit(solution)/shard_map/ppermute | solution.py:17
  36.1 8.8 %copy-start.5 = (bf16[8,1,3,3,3]{0,4,3,2,1:T(4,128)(2,1)S(1)}, bf16[8,1,3,3,3]{0,4,3,2,1:T(4,128)(2,1)}, u32[]{:S(2)}) copy-start(bf16[8,1,3,3,3]{0,4,3,2,1:T(4,128)(2,1)} %param.8) | copy-start | bytes 1300
  36.1 8.8 %copy-start.6 = (pred[8,17]{0,1:T(8,128)(4,1)S(1)}, pred[8,17]{0,1:T(8,128)(4,1)}, u32[]{:S(2)}) copy-start(pred[8,17]{0,1:T(8,128)(4,1)} %constant.41) | copy-start | bytes 412
  71.0 6.0 %copy-start.1 = (f32[8]{0:T(128)S(1)}, f32[8]{0:T(128)}, u32[]{:S(2)}) copy-start(f32[8]{0:T(128)} %param.9) | copy-start | bytes 100
  77.1 34.5 %collective-permute-start.4 = (bf16[8,1,16,128]{3,0,2,1:T(8,128)(2,1)S(1)}, bf16[8,1,16,128]{3,0,2,1:T(8,128)(2,1)S(1)}, u32[]{:S(2)}, u32[]{:S(2)}) collective-permute-start(bf16[8,1,16,128]{3,0,2,1:T(8,128)(2,1)S(1)} %slice.100), channel_id=1, source_target_pairs={{0,16},{16,32},{32,48},{48,64},{64,80},{80,96},{96,112},{112,128},... | collective-permute-start | bytes 98312 | tf_op jit(solution)/shard_map/ppermute | solution.py:15
  111.8 6.7 %collective-permute-start.5 = (bf16[8,1,16,128]{3,0,2,1:T(8,128)(2,1)S(1)}, bf16[8,1,16,128]{3,0,2,1:T(8,128)(2,1)S(1)}, u32[]{:S(2)}, u32[]{:S(2)}) collective-permute-start(bf16[8,1,16,128]{3,0,2,1:T(8,128)(2,1)S(1)} %slice.110), channel_id=1, source_target_pairs={{16,0},{32,16},{48,32},{64,48},{80,64},{96,80},{112,96},{128,112},... | collective-permute-start | bytes 98312 | tf_op jit(solution)/shard_map/ppermute | solution.py:17
  118.6 7.7 %collective-permute-start.6 = (bf16[8,18,1,128]{3,0,2,1:T(8,128)(2,1)S(1)}, bf16[8,18,1,128]{3,0,2,1:T(8,128)(2,1)S(1)}, u32[]{:S(2)}, u32[]{:S(2)}) collective-permute-start(bf16[8,18,1,128]{3,0,2,1:T(8,128)(2,1)S(1)} %get-tuple-element.11), channel_id=1, source_target_pairs={{0,1},{1,2},{2,3},{3,4},{4,5},{5,6},{6,7},{7,8},{8,9},{9,10},{10,1... | collective-permute-start | bytes 110600 | tf_op jit(solution)/shard_map/ppermute | solution.py:15
  120.5 7.4 %collective-permute-start.7 = (bf16[8,18,1,128]{3,0,2,1:T(8,128)(2,1)S(1)}, bf16[8,18,1,128]{3,0,2,1:T(8,128)(2,1)S(1)}, u32[]{:S(2)}, u32[]{:S(2)}) collective-permute-start(bf16[8,18,1,128]{3,0,2,1:T(8,128)(2,1)S(1)} %get-tuple-element.12), channel_id=1, source_target_pairs={{1,0},{2,1},{3,2},{4,3},{5,4},{6,5},{7,6},{8,7},{9,8},{10,9},{11,1... | collective-permute-start | bytes 110600 | tf_op jit(solution)/shard_map/ppermute | solution.py:17
  228.5 6.6 %copy-start.2 = (f32[8]{0:T(128)S(1)}, f32[8]{0:T(128)}, u32[]{:S(2)}) copy-start(f32[8]{0:T(128)} %param.11) | copy-start | bytes 100
  236.3 7.7 %collective-permute-start.8 = (bf16[8,16,1,128]{3,0,2,1:T(8,128)(2,1)S(1)}, bf16[8,16,1,128]{3,0,2,1:T(8,128)(2,1)S(1)}, u32[]{:S(2)}, u32[]{:S(2)}) collective-permute-start(bf16[8,16,1,128]{3,0,2,1:T(8,128)(2,1)S(1)} %pad_maximum_fusion.5), channel_id=1, source_target_pairs={{0,1},{1,2},{2,3},{3,4},{4,5},{5,6},{6,7},{7,8},{8,9},{9,10},{10,1... | collective-permute-start | bytes 98312 | tf_op jit(solution)/shard_map/ppermute | solution.py:35
  244.1 8.8 %collective-permute-start.9 = (bf16[8,1,17,128]{3,0,2,1:T(8,128)(2,1)S(1)}, bf16[8,1,17,128]{3,0,2,1:T(8,128)(2,1)S(1)}, u32[]{:S(2)}, u32[]{:S(2)}) collective-permute-start(bf16[8,1,17,128]{3,0,2,1:T(8,128)(2,1)S(1)} %pad_maximum_fusion.1), channel_id=1, source_target_pairs={{0,16},{16,32},{32,48},{48,64},{64,80},{80,96},{96,112},{112,128},... | collective-permute-start | bytes 104456 | tf_op jit(solution)/shard_map/ppermute | solution.py:35
  259.1 20.3 %copy-start.4 = (bf16[16,8,3,3,3]{0,1,4,3,2:T(8,128)(2,1)S(1)}, bf16[16,8,3,3,3]{0,1,4,3,2:T(8,128)(2,1)}, u32[]{:S(2)}) copy-start(bf16[16,8,3,3,3]{0,1,4,3,2:T(8,128)(2,1)} %param.12) | copy-start | bytes 20740
  259.1 20.3 %copy-start.7 = (pred[8,9]{0,1:T(8,128)(4,1)S(1)}, pred[8,9]{0,1:T(8,128)(4,1)}, u32[]{:S(2)}) copy-start(pred[8,9]{0,1:T(8,128)(4,1)} %constant.40) | copy-start | bytes 220
  291.1 1.0 copy-start.3
where the time goes:
time: 297 us; the launch traced here: 293 us
  local copies, waits for them, and re-layouts  131 us (44%)
  matrix products  86 us (29%)
  starting transfers between devices  38.5 us (13%)
  waiting for transfers between devices  19 us (6%)
  blocking collectives  10.6 us (4%)
  other arithmetic  7.4 us (2%)
    conv_general_dilated x40, local copies, waits for them, and re-layouts, conv_layer(): lax.conv_general_dilated(section[None], kernel, (1, 1, 1), ((0, 0), (0, 0...  101 us
    conv_general_dilated x8, matrix products, conv_layer(): lax.conv_general_dilated(section[None], kernel, (1, 1, 1), ((0, 0), (0, 0...  74.6 us
    conv_general_dilated x5, local copies, waits for them, and re-layouts, body(): lax.conv_general_dilated(extended[None], kernel_three, (2, 2, 2), ((0, 0)...  26.5 us
    ppermute x4, starting transfers between devices, extended_2(): lax.ppermute(head, axis, [((i + 1) % count, i) for i in range(ends)])  18.3 us
    ppermute x4, starting transfers between devices, extended_2(): lax.ppermute(tail, axis, [(i, (i + 1) % count) for i in range(ends)])  15.1 us
    ppermute x2, waiting for transfers between devices, from_behind(): return lax.ppermute(shard, axis, pairs)  11.5 us
    conv_general_dilated x1, matrix products, body(): lax.conv_general_dilated(extended[None], kernel_three, (2, 2, 2), ((0, 0)...  11.3 us
    all_to_all x1, blocking collectives, body(): lax.all_to_all(sky_cube.astype(jnp.bfloat16), 'tile', split_axis=1, conca...  10.6 us
  transfers between devices with their start and end apart: 10, of which 6 were waited for; matrix products, arithmetic and copies ran while one was open for 10% of the time, Pallas kernels for 0%

commit v1 on v0

--- a/solution.py
+++ b/solution.py
@@ -59,9 +59,11 @@
 
 
 def body(sky_cube, kernel_one, bias_one, kernel_two, bias_two, kernel_three, bias_three):
-    slab = lax.all_to_all(
-        sky_cube.astype(jnp.bfloat16), "tile", split_axis=1, concat_axis=0, tiled=True
-    )
+    x = sky_cube.astype(jnp.bfloat16)
+    n_dev = lax.axis_size("tile")
+    pieces = jnp.stack(jnp.split(x, n_dev, axis=1), axis=0)
+    pieces = lax.all_to_all(pieces, "tile", split_axis=0, concat_axis=0)
+    slab = jnp.concatenate(pieces, axis=0)
     widened = extended_2(slab, (("freq", 0), ("tile", 1)), 1)
     layer_one = conv_layer(widened[None], kernel_one, bias_one)
     widened = extended_2(layer_one, (("freq", 1), ("tile", 2)), 1)

time: 297 us -> 295 us (level)
  transfers between devices with their start and end apart: 10 -> 10, of which waited for: 6 -> 6; matrix products, arithmetic and copies ran while one was open for 10% -> 11% of each run, Pallas kernels for 0% -> 0%
where the time goes in v1:
time: 295 us; the launch traced here: 292 us
  local copies, waits for them, and re-layouts  130 us (44%)
  matrix products  86.2 us (29%)
  starting transfers between devices  38.5 us (13%)
  waiting for transfers between devices  19 us (6%)
  blocking collectives  10.6 us (4%)
  other arithmetic  6.38 us (2%)
    conv_general_dilated x40, local copies, waits for them, and re-layouts, conv_layer(): lax.conv_general_dilated(section[None], kernel, (1, 1, 1), ((0, 0), (0, 0...  101 us
    conv_general_dilated x8, matrix products, conv_layer(): lax.conv_general_dilated(section[None], kernel, (1, 1, 1), ((0, 0), (0, 0...  74.9 us
    conv_general_dilated x5, local copies, waits for them, and re-layouts, body(): lax.conv_general_dilated(extended[None], kernel_three, (2, 2, 2), ((0, 0)...  26.5 us
    ppermute x4, starting transfers between devices, extended_2(): lax.ppermute(head, axis, [((i + 1) % count, i) for i in range(ends)])  18.3 us
    ppermute x4, starting transfers between devices, extended_2(): lax.ppermute(tail, axis, [(i, (i + 1) % count) for i in range(ends)])  15 us
    ppermute x2, waiting for transfers between devices, from_behind(): return lax.ppermute(shard, axis, pairs)  11.5 us
    conv_general_dilated x1, matrix products, body(): lax.conv_general_dilated(extended[None], kernel_three, (2, 2, 2), ((0, 0)...  11.3 us
    all_to_all x1, blocking collectives, body(): pieces = lax.all_to_all(pieces, 'tile', split_axis=0, concat_axis=0)  10.6 us
  transfers between devices with their start and end apart: 10, of which 6 were waited for; matrix products, arithmetic and copies ran while one was open for 11% of the time, Pallas kernels for 0%

profile of v1, /device:TPU:34, one launch (start us, length us, event | category | flops | bytes accessed | tf_op | source)
XLA Modules:
  0.0 291.6 jit_solution(7645015074398607450)
XLA Ops:
  0.0 0.9 convert_element_type.30
  1.1 10.6 %all_to_all.5 = bf16[16,1,16,128]{3,2,1,0:T(8,128)(2,1)S(1)} all-to-all(bf16[16,1,16,128]{3,2,1,0:T(8,128)(2,1)S(1)} %constant_dynamic-update-slice_fusion), channel_id=1, replica_groups=mesh['freq'=16,'tile'=16] {'tile'}, dimensions={0} | all-to-all | bytes 131072 | tf_op jit(solution)/shard_map/all_to_all | solution.py:65
  11.7 5.2 %collective-permute-start = (bf16[1,16,128]{2,1,0:T(8,128)(2,1)S(1)}, bf16[1,16,128]{2,1,0:T(8,128)(2,1)S(1)}, u32[]{:S(2)}, u32[]{:S(2)}) collective-permute-start(bf16[1,16,128]{2,1,0:T(8,128)(2,1)S(1)} %get-tuple-element.19), channel_id=1, source_target_pairs={{0,16},{16,32},{32,48},{48,64},{64,80},{80,96},{96,112},{112,128},... | collective-permute-start | bytes 12296 | tf_op jit(solution)/shard_map/ppermute | solution.py:15
  16.9 4.0 %collective-permute-start.1 = (bf16[1,16,128]{2,1,0:T(8,128)(2,1)S(1)}, bf16[1,16,128]{2,1,0:T(8,128)(2,1)S(1)}, u32[]{:S(2)}, u32[]{:S(2)}) collective-permute-start(bf16[1,16,128]{2,1,0:T(8,128)(2,1)S(1)} %get-tuple-element.20), channel_id=1, source_target_pairs={{16,0},{32,16},{48,32},{64,48},{80,64},{96,80},{112,96},{128,112},... | collective-permute-start | bytes 12296 | tf_op jit(solution)/shard_map/ppermute | solution.py:17
  20.9 3.0 %collective-permute-done.1 = bf16[1,16,128]{2,1,0:T(8,128)(2,1)S(1)} collective-permute-done((bf16[1,16,128]{2,1,0:T(8,128)(2,1)S(1)}, bf16[1,16,128]{2,1,0:T(8,128)(2,1)S(1)}, u32[]{:S(2)}, u32[]{:S(2)}) %collective-permute-start.1) | collective-permute-done | bytes 4128 | tf_op jit(solution)/shard_map/ppermute | solution.py:17
  24.0 1.9 collective-permute-start.2
  25.9 5.8 %collective-permute-start.3 = (bf16[18,1,128]{2,1,0:T(2,128)(2,1)S(1)}, bf16[18,1,128]{2,1,0:T(2,128)(2,1)S(1)}, u32[]{:S(2)}, u32[]{:S(2)}) collective-permute-start(bf16[18,1,128]{2,1,0:T(2,128)(2,1)S(1)} %get-tuple-element.18), channel_id=1, source_target_pairs={{1,0},{2,1},{3,2},{4,3},{5,4},{6,5},{7,6},{8,7},{9,8},{10,9},{11,1... | collective-permute-start | bytes 13832 | tf_op jit(solution)/shard_map/ppermute | solution.py:17
  31.7 1.3 collective-permute-done.3
  35.3 2.2 copy.101
  37.4 2.6 copy.104
  40.0 1.6 copy.107
  41.6 1.7 copy.110
  43.3 8.7 %broadcast_select_fusion.4 = f32[4,16,8,17,8]{4,2,3,1,0:T(8,128)} fusion(pred[8,17]{0,1:T(8,128)(4,1)S(1)} %copy-done.6, bf16[1,6,18,8,19]{3,0,4,2,1:T(2,128)(2,1)S(1)} %copy.110, bf16[8,1,3,3,3]{0,4,3,2,1:T(4,128)(2,1)S(1)} %copy-done.5), kind=kOutput, calls=%fused_computation.39 | convolution fusion | flops 3829760 | bytes 311928 | tf_op jit(solution)/shard_map/conv_general_dilated | solution.py:48
  52.0 8.8 %broadcast_select_fusion.5 = f32[4,16,8,17,8]{4,2,3,1,0:T(8,128)} fusion(pred[8,17]{0,1:T(8,128)(4,1)S(1)} %copy-done.6, bf16[1,6,18,8,19]{3,0,4,2,1:T(2,128)(2,1)S(1)} %copy.107, bf16[8,1,3,3,3]{0,4,3,2,1:T(4,128)(2,1)S(1)} %copy-done.5), kind=kOutput, calls=%fused_computation.40 | convolution fusion | flops 3829760 | bytes 311928 | tf_op jit(solution)/shard_map/conv_general_dilated | solution.py:48
  60.8 8.8 %broadcast_select_fusion.7 = f32[4,16,8,17,8]{4,2,3,1,0:T(8,128)} fusion(pred[8,17]{0,1:T(8,128)(4,1)S(1)} %copy-done.6, bf16[1,6,18,8,19]{3,0,4,2,1:T(2,128)(2,1)S(1)} %copy.101, bf16[8,1,3,3,3]{0,4,3,2,1:T(4,128)(2,1)S(1)} %copy-done.5), kind=kOutput, calls=%fused_computation.42 | convolution fusion | flops 3829760 | bytes 311928 | tf_op jit(solution)/shard_map/conv_general_dilated | solution.py:48
  69.5 5.4 %copy.103 = f32[4,16,8,17,8]{3,2,4,1,0:T(8,128)S(1)} copy(f32[4,16,8,17,8]{4,2,3,1,0:T(8,128)} %broadcast_select_fusion.7) | data formatting | bytes 557056 | tf_op jit(solution)/shard_map/conv_general_dilated | solution.py:48
  74.9 0.6 reshape.15
  75.6 6.0 %collective-permute-start.4 = (bf16[8,1,16,128]{3,0,2,1:T(8,128)(2,1)S(1)}, bf16[8,1,16,128]{3,0,2,1:T(8,128)(2,1)S(1)}, u32[]{:S(2)}, u32[]{:S(2)}) collective-permute-start(bf16[8,1,16,128]{3,0,2,1:T(8,128)(2,1)S(1)} %slice.103), channel_id=1, source_target_pairs={{0,16},{16,32},{32,48},{48,64},{64,80},{80,96},{96,112},{112,128},... | collective-permute-start | bytes 98312 | tf_op jit(solution)/shard_map/ppermute | solution.py:15
  81.7 9.6 %broadcast_select_fusion.6 = f32[4,16,8,17,8]{4,2,3,1,0:T(8,128)} fusion(pred[8,17]{0,1:T(8,128)(4,1)S(1)} %copy-done.6, bf16[1,6,18,8,19]{3,0,4,2,1:T(2,128)(2,1)} %copy.104, bf16[8,1,3,3,3]{0,4,3,2,1:T(4,128)(2,1)S(1)} %copy-done.5), kind=kOutput, calls=%fused_computation.41 | convolution fusion | flops 3829760 | bytes 311928 | tf_op jit(solution)/shard_map/conv_general_dilated | solution.py:48
  91.3 5.2 %copy.112 = f32[4,16,8,17,8]{3,2,4,1,0:T(8,128)S(1)} copy(f32[4,16,8,17,8]{4,2,3,1,0:T(8,128)} %broadcast_select_fusion.4) | data formatting | bytes 557056 | tf_op jit(solution)/shard_map/conv_general_dilated | solution.py:48
  96.4 1.4 reshape.36
  97.8 5.2 %copy.109 = f32[4,16,8,17,8]{3,2,4,1,0:T(8,128)S(1)} copy(f32[4,16,8,17,8]{4,2,3,1,0:T(8,128)} %broadcast_select_fusion.5) | data formatting | bytes 557056 | tf_op jit(solution)/shard_map/conv_general_dilated | solution.py:48
  103.0 1.4 reshape.29
  104.4 5.2 %copy.106 = f32[4,16,8,17,8]{3,2,4,1,0:T(8,128)S(1)} copy(f32[4,16,8,17,8]{4,2,3,1,0:T(8,128)} %broadcast_select_fusion.6) | data formatting | bytes 557056 | tf_op jit(solution)/shard_map/conv_general_dilated | solution.py:48
  110.3 2.8 collective-permute-start.5
  113.1 1.1 fusion.83
  114.2 1.1 fusion.82
  115.4 1.6 collective-permute-done.5
  117.1 1.9 collective-permute-start.6
  119.0 5.8 %collective-permute-start.7 = (bf16[8,18,1,128]{3,0,2,1:T(8,128)(2,1)S(1)}, bf16[8,18,1,128]{3,0,2,1:T(8,128)(2,1)S(1)}, u32[]{:S(2)}, u32[]{:S(2)}) collective-permute-start(bf16[8,18,1,128]{3,0,2,1:T(8,128)(2,1)S(1)} %get-tuple-element.12), channel_id=1, source_target_pairs={{1,0},{2,1},{3,2},{4,3},{5,4},{6,5},{7,6},{8,7},{9,8},{10,9},{11,1... | collective-permute-start | bytes 110600 | tf_op jit(solution)/shard_map/ppermute | solution.py:17
  124.8 1.6 collective-permute-done.7
  127.3 2.5 reshape.46
  129.8 2.2 reshape.53
  132.0 2.3 reshape.60
  134.3 1.3 reshape.39
  135.6 6.6 %copy.114 = bf16[8,6,18,1,8,17]{0,4,5,2,1,3:T(8,128)(2,1)} copy(bf16[8,6,18,1,8,17]{5,4,0,2,1,3:T(8,128)(2,1)S(1)} %reshape.39) | data formatting | bytes 470016 | tf_op jit(solution)/shard_map/conv_general_dilated | solution.py:48
  142.2 1.1 slice.117
  143.4 9.8 %broadcast_select_fusion.3 = f32[4,16,8,17,8]{4,2,3,1,0:T(8,128)} fusion(pred[8,17]{0,1:T(8,128)(4,1)S(1)} %copy-done.6, bf16[8,8,3,3,3]{1,0,4,3,2:T(8,128)(2,1)S(1)} %copy-done, bf16[8,6,18,1,7,2]{0,4,5,2,1,3:T(8,128)(2,1)S(1)} %slice.117, bf16[8,6,18,1,8,17]{0,4,5,2,1,3:T(8,128)(2,1)} %copy.114), kind=kOutput, calls=%fused_computation.38 | convolution fusion | flops 30938624 | bytes 541320 | tf_op jit(solution)/shard_map/conv_general_dilated | solution.py:48
  153.2 5.2 %copy.115 = f32[4,16,8,17,8]{3,2,4,1,0:T(8,128)S(1)} copy(f32[4,16,8,17,8]{4,2,3,1,0:T(8,128)} %broadcast_select_fusion.3) | data formatting | bytes 557056 | tf_op jit(solution)/shard_map/conv_general_dilated | solution.py:48
  158.9 7.5 %copy.123 = bf16[8,6,18,1,8,17]{0,4,5,2,1,3:T(8,128)(2,1)} copy(bf16[8,6,18,1,8,17]{5,4,0,2,1,3:T(8,128)(2,1)} %reshape.60) | data formatting | bytes 470016 | tf_op jit(solution)/shard_map/conv_general_dilated | solution.py:48
  166.4 1.1 slice.126
  167.6 9.8 %broadcast_select_fusion = f32[4,16,8,17,8]{4,2,3,1,0:T(8,128)} fusion(pred[8,17]{0,1:T(8,128)(4,1)S(1)} %copy-done.6, bf16[8,8,3,3,3]{1,0,4,3,2:T(8,128)(2,1)S(1)} %copy-done, bf16[8,6,18,1,7,2]{0,4,5,2,1,3:T(8,128)(2,1)S(1)} %slice.126, bf16[8,6,18,1,8,17]{0,4,5,2,1,3:T(8,128)(2,1)} %copy.123), kind=kOutput, calls=%fused_computation.35 | convolution fusion | flops 30938624 | bytes 541320 | tf_op jit(solution)/shard_map/conv_general_dilated | solution.py:48
  177.4 5.6 %copy.124 = f32[4,16,8,17,8]{3,2,4,1,0:T(8,128)S(1)} copy(f32[4,16,8,17,8]{4,2,3,1,0:T(8,128)} %broadcast_select_fusion) | data formatting | bytes 557056 | tf_op jit(solution)/shard_map/conv_general_dilated | solution.py:48
  183.5 7.5 %copy.120 = bf16[8,6,18,1,8,17]{0,4,5,2,1,3:T(8,128)(2,1)} copy(bf16[8,6,18,1,8,17]{5,4,0,2,1,3:T(8,128)(2,1)} %reshape.53) | data formatting | bytes 470016 | tf_op jit(solution)/shard_map/conv_general_dilated | solution.py:48
  191.1 1.1 slice.123
  192.2 9.8 %broadcast_select_fusion.1 = f32[4,16,8,17,8]{4,2,3,1,0:T(8,128)} fusion(pred[8,17]{0,1:T(8,128)(4,1)S(1)} %copy-done.6, bf16[8,8,3,3,3]{1,0,4,3,2:T(8,128)(2,1)S(1)} %copy-done, bf16[8,6,18,1,7,2]{0,4,5,2,1,3:T(8,128)(2,1)S(1)} %slice.123, bf16[8,6,18,1,8,17]{0,4,5,2,1,3:T(8,128)(2,1)} %copy.120), kind=kOutput, calls=%fused_computation.36 | convolution fusion | flops 30938624 | bytes 541320 | tf_op jit(solution)/shard_map/conv_general_dilated | solution.py:48
  202.0 5.2 %copy.121 = f32[4,16,8,17,8]{3,2,4,1,0:T(8,128)S(1)} copy(f32[4,16,8,17,8]{4,2,3,1,0:T(8,128)} %broadcast_select_fusion.1) | data formatting | bytes 557056 | tf_op jit(solution)/shard_map/conv_general_dilated | solution.py:48
  207.2 1.4 reshape.57
  208.6 7.5 %copy.117 = bf16[8,6,18,1,8,17]{0,4,5,2,1,3:T(8,128)(2,1)} copy(bf16[8,6,18,1,8,17]{5,4,0,2,1,3:T(8,128)(2,1)} %reshape.46) | data formatting | bytes 470016 | tf_op jit(solution)/shard_map/conv_general_dilated | solution.py:48
  216.1 1.1 slice.120
  217.2 9.8 %broadcast_select_fusion.2 = f32[4,16,8,17,8]{4,2,3,1,0:T(8,128)} fusion(pred[8,17]{0,1:T(8,128)(4,1)S(1)} %copy-done.6, bf16[8,8,3,3,3]{1,0,4,3,2:T(8,128)(2,1)S(1)} %copy-done, bf16[8,6,18,1,7,2]{0,4,5,2,1,3:T(8,128)(2,1)S(1)} %slice.120, bf16[8,6,18,1,8,17]{0,4,5,2,1,3:T(8,128)(2,1)} %copy.117), kind=kOutput, calls=%fused_computation.37 | convolution fusion | flops 30938624 | bytes 541320 | tf_op jit(solution)/shard_map/conv_general_dilated | solution.py:48
  227.0 5.2 %copy.118 = f32[4,16,8,17,8]{3,2,4,1,0:T(8,128)S(1)} copy(f32[4,16,8,17,8]{4,2,3,1,0:T(8,128)} %broadcast_select_fusion.2) | data formatting | bytes 557056 | tf_op jit(solution)/shard_map/conv_general_dilated | solution.py:48
  232.2 1.4 reshape.50
  233.6 1.3 fusion.62
  234.8 1.9 collective-permute-start.8
  236.8 5.8 %collective-permute-done.8 = bf16[8,16,1,128]{3,0,2,1:T(8,128)(2,1)S(1)} collective-permute-done((bf16[8,16,1,128]{3,0,2,1:T(8,128)(2,1)S(1)}, bf16[8,16,1,128]{3,0,2,1:T(8,128)(2,1)S(1)}, u32[]{:S(2)}, u32[]{:S(2)}) %collective-permute-start.8) | collective-permute-done | bytes 32800 | tf_op jit(solution)/shard_map/ppermute | solution.py:35
  242.6 3.2 %collective-permute-start.9 = (bf16[8,1,17,128]{3,0,2,1:T(8,128)(2,1)S(1)}, bf16[8,1,17,128]{3,0,2,1:T(8,128)(2,1)S(1)}, u32[]{:S(2)}, u32[]{:S(2)}) collective-permute-start(bf16[8,1,17,128]{3,0,2,1:T(8,128)(2,1)S(1)} %pad_maximum_fusion.1), channel_id=1, source_target_pairs={{0,16},{16,32},{32,48},{48,64},{64,80},{80,96},{96,112},{112,128},... | collective-permute-start | bytes 104456 | tf_op jit(solution)/shard_map/ppermute | solution.py:35
  245.8 5.7 %collective-permute-done.9 = bf16[8,1,17,128]{3,0,2,1:T(8,128)(2,1)S(1)} collective-permute-done((bf16[8,1,17,128]{3,0,2,1:T(8,128)(2,1)S(1)}, bf16[8,1,17,128]{3,0,2,1:T(8,128)(2,1)S(1)}, u32[]{:S(2)}, u32[]{:S(2)}) %collective-permute-start.9) | collective-permute-done | bytes 34848 | tf_op jit(solution)/shard_map/ppermute | solution.py:35
  251.9 5.7 %reshape.67 = bf16[8,17,17,1,8,18]{5,4,0,2,1,3:T(8,128)(2,1)} reshape(bf16[8,17,17,1,144]{4,0,2,1,3:T(8,128)(2,1)S(1)} %pad.16) | data formatting | bytes 1331712 | tf_op jit(solution)/shard_map/conv_general_dilated | solution.py:75
  257.6 18.6 %copy.126 = bf16[8,17,17,1,8,18]{0,4,5,2,1,3:T(8,128)(2,1)} copy(bf16[8,17,17,1,8,18]{5,4,0,2,1,3:T(8,128)(2,1)} %reshape.67) | data formatting | bytes 1331712 | tf_op jit(solution)/shard_map/conv_general_dilated | solution.py:75
  276.2 1.6 slice.128
  277.8 11.3 %fusion.50 = f32[8,8,8,9,16]{4,2,3,1,0:T(8,128)S(1)} fusion(bf16[16,8,3,3,3]{0,1,4,3,2:T(8,128)(2,1)S(1)} %copy-done.4, bf16[8,17,17,1,7,2]{0,4,5,2,1,3:T(8,128)(2,1)S(1)} %slice.128, bf16[8,17,17,1,8,18]{0,4,5,2,1,3:T(8,128)(2,1)} %copy.126, pred[8,9]{0,1:T(8,128)(4,1)S(1)} %copy-done.7), kind=kOutput, calls=%fused_computation.47 | convolution fusion | flops 34143744 | bytes 1032488 | tf_op jit(solution)/shard_map/conv_general_dilated | solution.py:75
  289.8 0.8 copy.129
  290.6 0.8 fusion.53
  (79 shorter events, 6.4 us)
Async XLA Ops:
  0.0 143.4 %copy-start = (bf16[8,8,3,3,3]{1,0,4,3,2:T(8,128)(2,1)S(1)}, bf16[8,8,3,3,3]{1,0,4,3,2:T(8,128)(2,1)}, u32[]{:S(2)}) copy-start(bf16[8,8,3,3,3]{1,0,4,3,2:T(8,128)(2,1)} %param.10) | copy-start | bytes 10372
  11.7 9.2 %collective-permute-start = (bf16[1,16,128]{2,1,0:T(8,128)(2,1)S(1)}, bf16[1,16,128]{2,1,0:T(8,128)(2,1)S(1)}, u32[]{:S(2)}, u32[]{:S(2)}) collective-permute-start(bf16[1,16,128]{2,1,0:T(8,128)(2,1)S(1)} %get-tuple-element.19), channel_id=1, source_target_pairs={{0,16},{16,32},{32,48},{48,64},{64,80},{80,96},{96,112},{112,128},... | collective-permute-start | bytes 12296 | tf_op jit(solution)/shard_map/ppermute | solution.py:15
  16.9 7.1 %collective-permute-start.1 = (bf16[1,16,128]{2,1,0:T(8,128)(2,1)S(1)}, bf16[1,16,128]{2,1,0:T(8,128)(2,1)S(1)}, u32[]{:S(2)}, u32[]{:S(2)}) collective-permute-start(bf16[1,16,128]{2,1,0:T(8,128)(2,1)S(1)} %get-tuple-element.20), channel_id=1, source_target_pairs={{16,0},{32,16},{48,32},{64,48},{80,64},{96,80},{112,96},{128,112},... | collective-permute-start | bytes 12296 | tf_op jit(solution)/shard_map/ppermute | solution.py:17
  24.0 7.7 %collective-permute-start.2 = (bf16[18,1,128]{2,1,0:T(2,128)(2,1)S(1)}, bf16[18,1,128]{2,1,0:T(2,128)(2,1)S(1)}, u32[]{:S(2)}, u32[]{:S(2)}) collective-permute-start(bf16[18,1,128]{2,1,0:T(2,128)(2,1)S(1)} %get-tuple-element.17), channel_id=1, source_target_pairs={{0,1},{1,2},{2,3},{3,4},{4,5},{5,6},{6,7},{7,8},{8,9},{9,10},{10,1... | collective-permute-start | bytes 13832 | tf_op jit(solution)/shard_map/ppermute | solution.py:15
  25.9 7.1 %collective-permute-start.3 = (bf16[18,1,128]{2,1,0:T(2,128)(2,1)S(1)}, bf16[18,1,128]{2,1,0:T(2,128)(2,1)S(1)}, u32[]{:S(2)}, u32[]{:S(2)}) collective-permute-start(bf16[18,1,128]{2,1,0:T(2,128)(2,1)S(1)} %get-tuple-element.18), channel_id=1, source_target_pairs={{1,0},{2,1},{3,2},{4,3},{5,4},{6,5},{7,6},{8,7},{9,8},{10,9},{11,1... | collective-permute-start | bytes 13832 | tf_op jit(solution)/shard_map/ppermute | solution.py:17
  34.5 8.8 %copy-start.5 = (bf16[8,1,3,3,3]{0,4,3,2,1:T(4,128)(2,1)S(1)}, bf16[8,1,3,3,3]{0,4,3,2,1:T(4,128)(2,1)}, u32[]{:S(2)}) copy-start(bf16[8,1,3,3,3]{0,4,3,2,1:T(4,128)(2,1)} %param.8) | copy-start | bytes 1300
  34.5 8.8 %copy-start.6 = (pred[8,17]{0,1:T(8,128)(4,1)S(1)}, pred[8,17]{0,1:T(8,128)(4,1)}, u32[]{:S(2)}) copy-start(pred[8,17]{0,1:T(8,128)(4,1)} %constant.41) | copy-start | bytes 412
  69.5 6.0 %copy-start.1 = (f32[8]{0:T(128)S(1)}, f32[8]{0:T(128)}, u32[]{:S(2)}) copy-start(f32[8]{0:T(128)} %param.9) | copy-start | bytes 100
  75.6 34.5 %collective-permute-start.4 = (bf16[8,1,16,128]{3,0,2,1:T(8,128)(2,1)S(1)}, bf16[8,1,16,128]{3,0,2,1:T(8,128)(2,1)S(1)}, u32[]{:S(2)}, u32[]{:S(2)}) collective-permute-start(bf16[8,1,16,128]{3,0,2,1:T(8,128)(2,1)S(1)} %slice.103), channel_id=1, source_target_pairs={{0,16},{16,32},{32,48},{48,64},{64,80},{80,96},{96,112},{112,128},... | collective-permute-start | bytes 98312 | tf_op jit(solution)/shard_map/ppermute | solution.py:15
  110.3 6.7 %collective-permute-start.5 = (bf16[8,1,16,128]{3,0,2,1:T(8,128)(2,1)S(1)}, bf16[8,1,16,128]{3,0,2,1:T(8,128)(2,1)S(1)}, u32[]{:S(2)}, u32[]{:S(2)}) collective-permute-start(bf16[8,1,16,128]{3,0,2,1:T(8,128)(2,1)S(1)} %slice.113), channel_id=1, source_target_pairs={{16,0},{32,16},{48,32},{64,48},{80,64},{96,80},{112,96},{128,112},... | collective-permute-start | bytes 98312 | tf_op jit(solution)/shard_map/ppermute | solution.py:17
  117.1 7.7 %collective-permute-start.6 = (bf16[8,18,1,128]{3,0,2,1:T(8,128)(2,1)S(1)}, bf16[8,18,1,128]{3,0,2,1:T(8,128)(2,1)S(1)}, u32[]{:S(2)}, u32[]{:S(2)}) collective-permute-start(bf16[8,18,1,128]{3,0,2,1:T(8,128)(2,1)S(1)} %get-tuple-element.11), channel_id=1, source_target_pairs={{0,1},{1,2},{2,3},{3,4},{4,5},{5,6},{6,7},{7,8},{8,9},{9,10},{10,1... | collective-permute-start | bytes 110600 | tf_op jit(solution)/shard_map/ppermute | solution.py:15
  119.0 7.4 %collective-permute-start.7 = (bf16[8,18,1,128]{3,0,2,1:T(8,128)(2,1)S(1)}, bf16[8,18,1,128]{3,0,2,1:T(8,128)(2,1)S(1)}, u32[]{:S(2)}, u32[]{:S(2)}) collective-permute-start(bf16[8,18,1,128]{3,0,2,1:T(8,128)(2,1)S(1)} %get-tuple-element.12), channel_id=1, source_target_pairs={{1,0},{2,1},{3,2},{4,3},{5,4},{6,5},{7,6},{8,7},{9,8},{10,9},{11,1... | collective-permute-start | bytes 110600 | tf_op jit(solution)/shard_map/ppermute | solution.py:17
  227.0 6.6 %copy-start.2 = (f32[8]{0:T(128)S(1)}, f32[8]{0:T(128)}, u32[]{:S(2)}) copy-start(f32[8]{0:T(128)} %param.11) | copy-start | bytes 100
  234.8 7.7 %collective-permute-start.8 = (bf16[8,16,1,128]{3,0,2,1:T(8,128)(2,1)S(1)}, bf16[8,16,1,128]{3,0,2,1:T(8,128)(2,1)S(1)}, u32[]{:S(2)}, u32[]{:S(2)}) collective-permute-start(bf16[8,16,1,128]{3,0,2,1:T(8,128)(2,1)S(1)} %pad_maximum_fusion.5), channel_id=1, source_target_pairs={{0,1},{1,2},{2,3},{3,4},{4,5},{5,6},{6,7},{7,8},{8,9},{9,10},{10,1... | collective-permute-start | bytes 98312 | tf_op jit(solution)/shard_map/ppermute | solution.py:35
  242.6 8.8 %collective-permute-start.9 = (bf16[8,1,17,128]{3,0,2,1:T(8,128)(2,1)S(1)}, bf16[8,1,17,128]{3,0,2,1:T(8,128)(2,1)S(1)}, u32[]{:S(2)}, u32[]{:S(2)}) collective-permute-start(bf16[8,1,17,128]{3,0,2,1:T(8,128)(2,1)S(1)} %pad_maximum_fusion.1), channel_id=1, source_target_pairs={{0,16},{16,32},{32,48},{48,64},{64,80},{80,96},{96,112},{112,128},... | collective-permute-start | bytes 104456 | tf_op jit(solution)/shard_map/ppermute | solution.py:35
  257.6 20.2 %copy-start.4 = (bf16[16,8,3,3,3]{0,1,4,3,2:T(8,128)(2,1)S(1)}, bf16[16,8,3,3,3]{0,1,4,3,2:T(8,128)(2,1)}, u32[]{:S(2)}) copy-start(bf16[16,8,3,3,3]{0,1,4,3,2:T(8,128)(2,1)} %param.12) | copy-start | bytes 20740
  257.6 20.2 %copy-start.7 = (pred[8,9]{0,1:T(8,128)(4,1)S(1)}, pred[8,9]{0,1:T(8,128)(4,1)}, u32[]{:S(2)}) copy-start(pred[8,9]{0,1:T(8,128)(4,1)} %constant.40) | copy-start | bytes 220
  289.6 1.0 copy-start.3
